TPU v7x, 32 devices: a whole 2x2x4 slice. The times are simulated.
32 devices in a mesh: lat: 4 (over y, x), lon: 8 (over z, core).
Axes of the slice: x: 2, y: 2, z: 4, core: 2. Of those that a mesh axis runs over, the one named last changes fastest.
Arguments:
- right_side: float32 [512, 2048], P('lat', 'lon'), may hold values from -12 to 12
- diagonal: float32 [512, 2048], P('lat', 'lon'), may hold values from 0.2 to 2
- east_coef: float32 [512, 2048], P('lat', 'lon'), may hold values from 0.5 to 2
- north_coef: float32 [512, 2048], P('lat', 'lon'), may hold values from 0.5 to 2
- land_sea: int32 [512, 2048], P('lat', 'lon'), may hold values 0 or 1
- fold_partner: int32 [2048], P('lon'), may hold values from 0 to 2047, as said below
Outputs:
- solution_field: float32 [512, 2048], P('lat', 'lon')
- residual: float32 [512, 2048], P('lat', 'lon')
Inputs may be any that keep to these rules, and one draw needn't show every extreme that they name: fold_partner[fold_partner[i]] = i and fold_partner[i] != i for every column i, and fold_partner[i] // 256 = 7 - i // 256.
All inputs are finite; a program needn't handle non-finite values. No bound on the sum of `land_sea` on one device may be relied on, other than what follows from the above.
Results may differ from a plain program's by a relative error of at most 0.00019.
Values sent between devices are 32-bit elements; how exact they have to be, the bound alone decides.
A program may use at most 64 MiB of HBM per device.

v0:
```python
import jax
import jax.numpy as jnp
from jax import lax
from jax.sharding import PartitionSpec as P

ITERS = 4


def with_halo(cells, sides, width, closed):
    for axis, dim in sides:
        count = lax.axis_size(axis)
        ends = count if closed else count - 1
        head = lax.slice_in_dim(cells, 0, width, axis=dim)
        tail = lax.slice_in_dim(cells, cells.shape[dim] - width, cells.shape[dim], axis=dim)
        cells = jnp.concatenate(
            [
                lax.ppermute(tail, axis, [(i, (i + 1) % count) for i in range(ends)]),
                cells,
                lax.ppermute(head, axis, [((i + 1) % count, i) for i in range(ends)]),
            ],
            axis=dim,
        )
    return cells


def zonal_rim(values):
    return with_halo(values, (("lon", 1),), 1, True)


def meridional_rim(values):
    return with_halo(values, (("lat", 0),), 1, False)


def paired(residual, image):
    return lax.psum((jnp.sum(residual * residual), jnp.sum(residual * image)), ("lat", "lon"))


def local(right_side, diagonal, east_coef, north_coef, land_sea, fold_partner):
    row_count, col_count = right_side.shape
    ocean = land_sea.astype(jnp.float32)
    on_top = lax.axis_index("lat") == lax.axis_size("lat") - 1
    row_ids = lax.broadcasted_iota(jnp.int32, (row_count, col_count), 0)
    north_inner = jnp.where(on_top & (row_ids == row_count - 1), 0.0, north_coef)
    west_coef = zonal_rim(east_coef)[:, :col_count]
    south_coef = meridional_rim(north_inner)[:row_count]

    def neighbours(masked):
        across_lon = zonal_rim(masked)
        across_lat = meridional_rim(masked)
        return (
            across_lon[:, 2:],
            across_lon[:, :col_count],
            across_lat[2:],
            across_lat[:row_count],
        )

    def mirror_row(top_values):
        whole_row = lax.all_gather(top_values, "lon", axis=0, tiled=True)
        return jnp.take(whole_row, fold_partner, axis=0)

    top_coef = north_coef[row_count - 1]
    fold_coef = jnp.where(on_top, 0.5 * (top_coef + mirror_row(top_coef)), 0.0)

    def operate(surface):
        masked = ocean * surface
        east_vals, west_vals, north_vals, south_vals = neighbours(masked)
        spread = east_coef * (masked - east_vals) + west_coef * (masked - west_vals)
        spread = spread + north_inner * (masked - north_vals) + south_coef * (masked - south_vals)
        last_row = masked[row_count - 1]
        spread = spread.at[row_count - 1].add(fold_coef * (last_row - mirror_row(last_row)))
        return diagonal * surface + ocean * spread

    solution_field = jnp.zeros_like(right_side)
    residual = right_side
    image = operate(residual)
    norm_now, product = paired(residual, image)
    alpha = norm_now / product
    direction, along = (residual, image)
    for iteration in range(ITERS):
        solution_field = solution_field + alpha * direction
        residual = residual - alpha * along
        if iteration + 1 < ITERS:
            image = operate(residual)
            norm_next, product = paired(residual, image)
            ratio = norm_next / norm_now
            alpha = norm_next / (product - ratio * norm_next / alpha)
            direction = residual + ratio * direction
            along = image + ratio * along
            norm_now = norm_next
    return (solution_field, residual)


def solution(mesh):
    placed = (
        P("lat", "lon"),
        P("lat", "lon"),
        P("lat", "lon"),
        P("lat", "lon"),
        P("lat", "lon"),
        P("lon"),
    )
    return jax.shard_map(
        local,
        mesh=mesh,
        in_specs=placed,
        out_specs=(P("lat", "lon"), P("lat", "lon")),
        check_vma=False,
    )
```

profile of v0, /device:TPU:12, one launch (start us, length us, event | category | flops | bytes accessed | tf_op | source)
XLA Modules:
  0.0 291.9 jit_solution(6611212178361798222)
XLA Ops:
  0.6 1.0 slice.203
  1.6 0.0 collective-permute-start.1
  1.7 0.0 copy-start
  1.7 0.0 copy-start.1
  1.7 0.1 broadcast_select_fusion
  1.8 3.4 %collective-permute-start.4 = (f32[1,256]{1,0:T(1,128)S(1)}, f32[1,256]{1,0:T(1,128)S(1)}, u32[]{:S(2)}, u32[]{:S(2)}) collective-permute-start(f32[1,256]{1,0:T(1,128)S(1)} %slice.255), channel_id=1, source_target_pairs={{0,8},{8,16},{16,24},{1,9},{9,17},{17,25},{2,10},{10,18},{18,26},{... | collective-permute-start | bytes 3080 | tf_op jit(solution)/shard_map/ppermute | solution.py:17
  5.3 3.3 %collective-permute-start.3 = (f32[1,256]{1,0:T(1,128)S(1)}, f32[1,256]{1,0:T(1,128)S(1)}, u32[]{:S(2)}, u32[]{:S(2)}) collective-permute-start(f32[1,256]{1,0:T(1,128)S(1)} %get-tuple-element.87), channel_id=1, source_target_pairs={{8,0},{16,8},{24,16},{9,1},{17,9},{25,17},{10,2},{18,10},{26,18},{... | collective-permute-start | bytes 3080 | tf_op jit(solution)/shard_map/ppermute | solution.py:19
  8.6 2.5 collective-permute-start.5
  11.1 0.1 fusion.57
  11.2 0.9 collective-permute-start
  12.1 10.8 %all-gather.1 = f32[1,2048]{1,0:T(1,128)S(1)} all-gather(f32[1,256]{1,0:T(1,128)S(1)} %get-tuple-element.88), channel_id=3, replica_groups=mesh['lat'=4,'lon'=8] {'lon'}, dimensions={1}, use_global_device_ids=true | all-gather | bytes 9216 | tf_op jit(solution)/shard_map/all_gather | solution.py:58
  22.9 10.2 %all-gather = f32[1,2048]{1,0:T(1,128)S(1)} all-gather(f32[1,256]{1,0:T(1,128)S(1)} %slice.214), channel_id=2, replica_groups=mesh['lat'=4,'lon'=8] {'lon'}, dimensions={1}, use_global_device_ids=true | all-gather | bytes 9216 | tf_op jit(solution)/shard_map/all_gather | solution.py:58
  33.1 1.7 gather_fusion
  34.8 0.0 copy-start.3
  34.8 1.7 gather_fusion.1
  36.6 0.0 collective-permute-done.1
  36.6 0.4 collective-permute-start.2
  37.0 0.0 collective-permute-done
  37.0 3.3 %collective-permute-done.2 = f32[128,1]{1,0:T(8,128)S(1)} collective-permute-done((f32[128,1]{1,0:T(8,128)S(1)}, f32[128,1]{1,0:T(8,128)S(1)}, u32[]{:S(2)}, u32[]{:S(2)}) %collective-permute-start.2) | collective-permute-done | bytes 544 | tf_op jit(solution)/shard_map/ppermute | solution.py:17
  40.3 0.2 fusion.35
  40.6 0.7 multiply_reduce_fusion.6
  41.3 41.4 %all-reduce.3 = (f32[]{:T(128)}, f32[]{:T(128)}) all-reduce(f32[]{:T(128)} %get-tuple-element.58, f32[]{:T(128)} %get-tuple-element.57), channel_id=1, replica_groups=mesh['lat'=4,'lon'=8] {'lat','lon'}, use_global_device_ids=true, to_apply=%region_1.2 | all-reduce | flops 2 | bytes 16 | tf_op jit(solution)/shard_map/psum | solution.py:35
  84.1 8.3 %all-gather.2 = f32[1,2048]{1,0:T(1,128)S(1)} all-gather(f32[1,256]{1,0:T(1,128)S(1)} %get-tuple-element.84), channel_id=4, replica_groups=mesh['lat'=4,'lon'=8] {'lon'}, dimensions={1}, use_global_device_ids=true | all-gather | bytes 9216 | tf_op jit(solution)/shard_map/all_gather | solution.py:58
  92.4 3.8 %collective-permute-start.9 = (f32[1,256]{1,0:T(1,128)S(1)}, f32[1,256]{1,0:T(1,128)S(1)}, u32[]{:S(2)}, u32[]{:S(2)}) collective-permute-start(f32[1,256]{1,0:T(1,128)S(1)} %get-tuple-element.84), channel_id=1, source_target_pairs={{0,8},{8,16},{16,24},{1,9},{9,17},{17,25},{2,10},{10,18},{18,26},{... | collective-permute-start | bytes 3080 | tf_op jit(solution)/shard_map/ppermute | solution.py:17
  96.2 0.1 fusion.55
  96.3 1.7 gather_fusion.2
  98.1 2.9 collective-permute-start.8
  101.0 1.5 collective-permute-start.6
  102.5 1.9 collective-permute-done.6
  104.4 1.8 collective-permute-done.7
  106.2 0.0 collective-permute-done.8
  106.2 0.0 collective-permute-done.9
  106.2 0.2 fusion.24
  106.5 0.7 multiply_reduce_fusion.4
  107.2 42.0 %all-reduce.2 = (f32[]{:T(128)}, f32[]{:T(128)}) all-reduce(f32[]{:T(128)} %get-tuple-element.54, f32[]{:T(128)} %get-tuple-element.53), channel_id=1, replica_groups=mesh['lat'=4,'lon'=8] {'lat','lon'}, use_global_device_ids=true, to_apply=%region_5.7 | all-reduce | flops 2 | bytes 16 | tf_op jit(solution)/shard_map/psum | solution.py:35
  153.8 0.1 convert_multiply_fusion.1
  153.9 8.1 %all-gather.3 = f32[1,2048]{1,0:T(1,128)S(1)} all-gather(f32[1,256]{1,0:T(1,128)S(1)} %get-tuple-element.80), channel_id=5, replica_groups=mesh['lat'=4,'lon'=8] {'lon'}, dimensions={1}, use_global_device_ids=true | all-gather | bytes 9216 | tf_op jit(solution)/shard_map/all_gather | solution.py:58
  162.0 2.8 collective-permute-start.13
  164.8 0.1 fusion.53
  164.9 1.7 gather_fusion.3
  166.6 3.9 %collective-permute-start.12 = (f32[1,256]{1,0:T(1,128)S(1)}, f32[1,256]{1,0:T(1,128)S(1)}, u32[]{:S(2)}, u32[]{:S(2)}) collective-permute-start(f32[1,256]{1,0:T(1,128)S(1)} %get-tuple-element.79), channel_id=1, source_target_pairs={{8,0},{16,8},{24,16},{9,1},{17,9},{25,17},{10,2},{18,10},{26,18},{... | collective-permute-start | bytes 3080 | tf_op jit(solution)/shard_map/ppermute | solution.py:19
  170.6 1.7 collective-permute-start.10
  172.3 0.0 collective-permute-start.11
  172.3 1.9 collective-permute-done.10
  174.2 1.8 collective-permute-done.11
  176.0 0.0 collective-permute-done.12
  176.0 0.0 collective-permute-done.13
  176.0 0.2 fusion.13
  176.2 0.7 multiply_reduce_fusion.2
  177.0 40.9 %all-reduce.1 = (f32[]{:T(128)}, f32[]{:T(128)}) all-reduce(f32[]{:T(128)} %get-tuple-element.52, f32[]{:T(128)} %get-tuple-element.51), channel_id=1, replica_groups=mesh['lat'=4,'lon'=8] {'lat','lon'}, use_global_device_ids=true, to_apply=%region_9.11 | all-reduce | flops 2 | bytes 16 | tf_op jit(solution)/shard_map/psum | solution.py:35
  221.8 0.1 convert_multiply_fusion
  221.9 8.2 %all-gather.4 = f32[1,2048]{1,0:T(1,128)S(1)} all-gather(f32[1,256]{1,0:T(1,128)S(1)} %get-tuple-element.76), channel_id=6, replica_groups=mesh['lat'=4,'lon'=8] {'lon'}, dimensions={1}, use_global_device_ids=true | all-gather | bytes 9216 | tf_op jit(solution)/shard_map/all_gather | solution.py:58
  230.1 3.8 %collective-permute-start.17 = (f32[1,256]{1,0:T(1,128)S(1)}, f32[1,256]{1,0:T(1,128)S(1)}, u32[]{:S(2)}, u32[]{:S(2)}) collective-permute-start(f32[1,256]{1,0:T(1,128)S(1)} %get-tuple-element.76), channel_id=1, source_target_pairs={{0,8},{8,16},{16,24},{1,9},{9,17},{17,25},{2,10},{10,18},{18,26},{... | collective-permute-start | bytes 3080 | tf_op jit(solution)/shard_map/ppermute | solution.py:17
  233.9 0.1 fusion.51
  234.0 1.7 gather_fusion.4
  235.7 2.9 collective-permute-start.16
  238.6 1.7 collective-permute-start.14
  240.3 1.9 collective-permute-done.14
  242.2 1.8 collective-permute-done.15
  244.0 0.0 collective-permute-done.17
  244.0 0.2 fusion.2
  244.3 0.7 multiply_reduce_fusion
  244.9 42.0 %all-reduce = (f32[]{:T(128)}, f32[]{:T(128)}) all-reduce(f32[]{:T(128)} %get-tuple-element.56, f32[]{:T(128)} %get-tuple-element.55), channel_id=1, replica_groups=mesh['lat'=4,'lon'=8] {'lat','lon'}, use_global_device_ids=true, to_apply=%region_13.15 | all-reduce | flops 2 | bytes 16 | tf_op jit(solution)/shard_map/psum | solution.py:35
  291.0 0.9 multiply_subtract_fusion
  (38 shorter events, 0.4 us)
Async XLA Ops:
  0.6 1.0 copy-start.4
  1.6 35.0 %collective-permute-start.1 = (f32[128,1]{1,0:T(8,128)S(1)}, f32[128,1]{1,0:T(8,128)S(1)}, u32[]{:S(2)}, u32[]{:S(2)}) collective-permute-start(f32[128,1]{1,0:T(8,128)S(1)} %slice.203), channel_id=1, source_target_pairs={{0,1},{1,2},{2,3},{3,4},{4,5},{5,6},{6,7},{7,0},{8,9},{9,10},{10,1... | collective-permute-start | bytes 1544 | tf_op jit(solution)/shard_map/ppermute | solution.py:17
  1.7 3.5 %copy-start = (s32[128,256]{1,0:T(8,128)S(1)}, s32[128,256]{1,0:T(8,128)}, u32[]{:S(2)}) copy-start(s32[128,256]{1,0:T(8,128)} %param.20) | copy-start | bytes 393220
  1.7 3.5 %copy-start.1 = (f32[128,256]{1,0:T(8,128)S(1)}, f32[128,256]{1,0:T(8,128)}, u32[]{:S(2)}) copy-start(f32[128,256]{1,0:T(8,128)} %param.16) | copy-start | bytes 393220
  1.8 38.5 %collective-permute-start.4 = (f32[1,256]{1,0:T(1,128)S(1)}, f32[1,256]{1,0:T(1,128)S(1)}, u32[]{:S(2)}, u32[]{:S(2)}) collective-permute-start(f32[1,256]{1,0:T(1,128)S(1)} %slice.255), channel_id=1, source_target_pairs={{0,8},{8,16},{16,24},{1,9},{9,17},{17,25},{2,10},{10,18},{18,26},{... | collective-permute-start | bytes 3080 | tf_op jit(solution)/shard_map/ppermute | solution.py:17
  5.3 35.0 %collective-permute-start.3 = (f32[1,256]{1,0:T(1,128)S(1)}, f32[1,256]{1,0:T(1,128)S(1)}, u32[]{:S(2)}, u32[]{:S(2)}) collective-permute-start(f32[1,256]{1,0:T(1,128)S(1)} %get-tuple-element.87), channel_id=1, source_target_pairs={{8,0},{16,8},{24,16},{9,1},{17,9},{25,17},{10,2},{18,10},{26,18},{... | collective-permute-start | bytes 3080 | tf_op jit(solution)/shard_map/ppermute | solution.py:19
  8.6 31.7 %collective-permute-start.5 = (f32[1,256]{1,0:T(1,128)S(1)}, f32[1,256]{1,0:T(1,128)S(1)}, u32[]{:S(2)}, u32[]{:S(2)}) collective-permute-start(f32[1,256]{1,0:T(1,128)S(1)} %get-tuple-element.88), channel_id=1, source_target_pairs={{0,8},{8,16},{16,24},{1,9},{9,17},{17,25},{2,10},{10,18},{18,26},{... | collective-permute-start | bytes 3080 | tf_op jit(solution)/shard_map/ppermute | solution.py:17
  11.2 25.8 %collective-permute-start = (f32[128,1]{1,0:T(8,128)S(1)}, f32[128,1]{1,0:T(8,128)S(1)}, u32[]{:S(2)}, u32[]{:S(2)}) collective-permute-start(f32[128,1]{1,0:T(8,128)S(1)} %get-tuple-element.85), channel_id=1, source_target_pairs={{1,0},{2,1},{3,2},{4,3},{5,4},{6,5},{7,6},{0,7},{9,8},{10,9},{11,1... | collective-permute-start | bytes 1544 | tf_op jit(solution)/shard_map/ppermute | solution.py:19
  12.1 10.8 %copy-start.5 = (s32[256]{0:T(256)S(1)}, s32[256]{0:T(256)}, u32[]{:S(2)}) copy-start(s32[256]{0:T(256)} %param.21) | copy-start | bytes 3076
  34.8 5.5 %copy-start.3 = (f32[128,256]{1,0:T(8,128)S(1)}, f32[128,256]{1,0:T(8,128)}, u32[]{:S(2)}) copy-start(f32[128,256]{1,0:T(8,128)} %param.18) | copy-start | bytes 393220
  36.6 3.7 %collective-permute-start.2 = (f32[128,1]{1,0:T(8,128)S(1)}, f32[128,1]{1,0:T(8,128)S(1)}, u32[]{:S(2)}, u32[]{:S(2)}) collective-permute-start(f32[128,1]{1,0:T(8,128)S(1)} %get-tuple-element.86), channel_id=1, source_target_pairs={{0,1},{1,2},{2,3},{3,4},{4,5},{5,6},{6,7},{7,0},{8,9},{9,10},{10,1... | collective-permute-start | bytes 1544 | tf_op jit(solution)/shard_map/ppermute | solution.py:17
  37.0 3.6 %copy-start.2 = (f32[128,256]{1,0:T(8,128)S(1)}, f32[128,256]{1,0:T(8,128)}, u32[]{:S(2)}) copy-start(f32[128,256]{1,0:T(8,128)} %param.17) | copy-start | bytes 393220
  92.4 13.8 %collective-permute-start.9 = (f32[1,256]{1,0:T(1,128)S(1)}, f32[1,256]{1,0:T(1,128)S(1)}, u32[]{:S(2)}, u32[]{:S(2)}) collective-permute-start(f32[1,256]{1,0:T(1,128)S(1)} %get-tuple-element.84), channel_id=1, source_target_pairs={{0,8},{8,16},{16,24},{1,9},{9,17},{17,25},{2,10},{10,18},{18,26},{... | collective-permute-start | bytes 3080 | tf_op jit(solution)/shard_map/ppermute | solution.py:17
  98.1 8.1 %collective-permute-start.8 = (f32[1,256]{1,0:T(1,128)S(1)}, f32[1,256]{1,0:T(1,128)S(1)}, u32[]{:S(2)}, u32[]{:S(2)}) collective-permute-start(f32[1,256]{1,0:T(1,128)S(1)} %get-tuple-element.83), channel_id=1, source_target_pairs={{8,0},{16,8},{24,16},{9,1},{17,9},{25,17},{10,2},{18,10},{26,18},{... | collective-permute-start | bytes 3080 | tf_op jit(solution)/shard_map/ppermute | solution.py:19
  101.0 3.4 %collective-permute-start.6 = (f32[128,1]{1,0:T(8,128)S(1)}, f32[128,1]{1,0:T(8,128)S(1)}, u32[]{:S(2)}, u32[]{:S(2)}) collective-permute-start(f32[128,1]{1,0:T(8,128)S(1)} %get-tuple-element.81), channel_id=1, source_target_pairs={{1,0},{2,1},{3,2},{4,3},{5,4},{6,5},{7,6},{0,7},{9,8},{10,9},{11,1... | collective-permute-start | bytes 1544 | tf_op jit(solution)/shard_map/ppermute | solution.py:19
  102.5 3.7 %collective-permute-start.7 = (f32[128,1]{1,0:T(8,128)S(1)}, f32[128,1]{1,0:T(8,128)S(1)}, u32[]{:S(2)}, u32[]{:S(2)}) collective-permute-start(f32[128,1]{1,0:T(8,128)S(1)} %get-tuple-element.82), channel_id=1, source_target_pairs={{0,1},{1,2},{2,3},{3,4},{4,5},{5,6},{6,7},{7,0},{8,9},{9,10},{10,1... | collective-permute-start | bytes 1544 | tf_op jit(solution)/shard_map/ppermute | solution.py:17
  162.0 14.0 %collective-permute-start.13 = (f32[1,256]{1,0:T(1,128)S(1)}, f32[1,256]{1,0:T(1,128)S(1)}, u32[]{:S(2)}, u32[]{:S(2)}) collective-permute-start(f32[1,256]{1,0:T(1,128)S(1)} %get-tuple-element.80), channel_id=1, source_target_pairs={{0,8},{8,16},{16,24},{1,9},{9,17},{17,25},{2,10},{10,18},{18,26},{... | collective-permute-start | bytes 3080 | tf_op jit(solution)/shard_map/ppermute | solution.py:17
  166.6 9.4 %collective-permute-start.12 = (f32[1,256]{1,0:T(1,128)S(1)}, f32[1,256]{1,0:T(1,128)S(1)}, u32[]{:S(2)}, u32[]{:S(2)}) collective-permute-start(f32[1,256]{1,0:T(1,128)S(1)} %get-tuple-element.79), channel_id=1, source_target_pairs={{8,0},{16,8},{24,16},{9,1},{17,9},{25,17},{10,2},{18,10},{26,18},{... | collective-permute-start | bytes 3080 | tf_op jit(solution)/shard_map/ppermute | solution.py:19
  170.6 3.6 %collective-permute-start.10 = (f32[128,1]{1,0:T(8,128)S(1)}, f32[128,1]{1,0:T(8,128)S(1)}, u32[]{:S(2)}, u32[]{:S(2)}) collective-permute-start(f32[128,1]{1,0:T(8,128)S(1)} %get-tuple-element.77), channel_id=1, source_target_pairs={{1,0},{2,1},{3,2},{4,3},{5,4},{6,5},{7,6},{0,7},{9,8},{10,9},{11,1... | collective-permute-start | bytes 1544 | tf_op jit(solution)/shard_map/ppermute | solution.py:19
  172.3 3.7 %collective-permute-start.11 = (f32[128,1]{1,0:T(8,128)S(1)}, f32[128,1]{1,0:T(8,128)S(1)}, u32[]{:S(2)}, u32[]{:S(2)}) collective-permute-start(f32[128,1]{1,0:T(8,128)S(1)} %get-tuple-element.78), channel_id=1, source_target_pairs={{0,1},{1,2},{2,3},{3,4},{4,5},{5,6},{6,7},{7,0},{8,9},{9,10},{10,1... | collective-permute-start | bytes 1544 | tf_op jit(solution)/shard_map/ppermute | solution.py:17
  230.1 13.9 %collective-permute-start.17 = (f32[1,256]{1,0:T(1,128)S(1)}, f32[1,256]{1,0:T(1,128)S(1)}, u32[]{:S(2)}, u32[]{:S(2)}) collective-permute-start(f32[1,256]{1,0:T(1,128)S(1)} %get-tuple-element.76), channel_id=1, source_target_pairs={{0,8},{8,16},{16,24},{1,9},{9,17},{17,25},{2,10},{10,18},{18,26},{... | collective-permute-start | bytes 3080 | tf_op jit(solution)/shard_map/ppermute | solution.py:17
  235.7 8.3 %collective-permute-start.16 = (f32[1,256]{1,0:T(1,128)S(1)}, f32[1,256]{1,0:T(1,128)S(1)}, u32[]{:S(2)}, u32[]{:S(2)}) collective-permute-start(f32[1,256]{1,0:T(1,128)S(1)} %get-tuple-element.75), channel_id=1, source_target_pairs={{8,0},{16,8},{24,16},{9,1},{17,9},{25,17},{10,2},{18,10},{26,18},{... | collective-permute-start | bytes 3080 | tf_op jit(solution)/shard_map/ppermute | solution.py:19
  238.6 3.6 %collective-permute-start.14 = (f32[128,1]{1,0:T(8,128)S(1)}, f32[128,1]{1,0:T(8,128)S(1)}, u32[]{:S(2)}, u32[]{:S(2)}) collective-permute-start(f32[128,1]{1,0:T(8,128)S(1)} %get-tuple-element.73), channel_id=1, source_target_pairs={{1,0},{2,1},{3,2},{4,3},{5,4},{6,5},{7,6},{0,7},{9,8},{10,9},{11,1... | collective-permute-start | bytes 1544 | tf_op jit(solution)/shard_map/ppermute | solution.py:19
  240.3 3.7 %collective-permute-start.15 = (f32[128,1]{1,0:T(8,128)S(1)}, f32[128,1]{1,0:T(8,128)S(1)}, u32[]{:S(2)}, u32[]{:S(2)}) collective-permute-start(f32[128,1]{1,0:T(8,128)S(1)} %get-tuple-element.74), channel_id=1, source_target_pairs={{0,1},{1,2},{2,3},{3,4},{4,5},{5,6},{6,7},{7,0},{8,9},{9,10},{10,1... | collective-permute-start | bytes 1544 | tf_op jit(solution)/shard_map/ppermute | solution.py:17
where the time goes:
time: 293 us; the launch traced here: 292 us
  blocking collectives  212 us (72%)
  starting transfers between devices  35.7 us (12%)
  between operations  14.9 us (5%)
  waiting for transfers between devices  14.4 us (5%)
  local copies, waits for them, and re-layouts  10.1 us (3%)
  other arithmetic  4.81 us (2%)
    psum x4, blocking collectives, paired(): lax.psum((jnp.sum(residual * residual), jnp.sum(residual * image)), ('lat...  166 us
    all_gather x5, blocking collectives, mirror_row(): whole_row = lax.all_gather(top_values, 'lon', axis=0, tiled=True)  45.7 us
    ppermute x8, starting transfers between devices, with_halo(): lax.ppermute(head, axis, [((i + 1) % count, i) for i in range(ends)])  18.9 us
    ppermute x10, starting transfers between devices, with_halo(): lax.ppermute(tail, axis, [(i, (i + 1) % count) for i in range(ends)])  16.8 us
    ppermute x10, waiting for transfers between devices, with_halo(): lax.ppermute(tail, axis, [(i, (i + 1) % count) for i in range(ends)])  8.69 us
    gather x5, local copies, waits for them, and re-layouts, mirror_row(): return jnp.take(whole_row, fold_partner, axis=0)  8.62 us
  transfers between devices with their start and end apart: 18, of which 7 were waited for; matrix products, arithmetic and copies ran while one was open for 3% of the time, Pallas kernels for 0%

commit v1 on v0

--- a/solution.py
+++ b/solution.py
@@ -4,6 +4,11 @@
 from jax.sharding import PartitionSpec as P
 
 ITERS = 4
+
+
+def by_each_axis(x, axis_one, axis_two):
+    half = lax.psum(x, axis_one)
+    return lax.psum(half, axis_two)
 
 
 def with_halo(cells, sides, width, closed):
@@ -32,7 +37,7 @@
 
 
 def paired(residual, image):
-    return lax.psum((jnp.sum(residual * residual), jnp.sum(residual * image)), ("lat", "lon"))
+    return by_each_axis((jnp.sum(residual * residual), jnp.sum(residual * image)), "lon", "lat")
 
 
 def local(right_side, diagonal, east_coef, north_coef, land_sea, fold_partner):

time: 293 us -> 230 us (0.78)
  the two profiles are of different devices: /device:TPU:12 before, /device:TPU:0 now
where the time goes in v1:
time: 230 us
  blocking collectives  148 us (64%)
  starting transfers between devices  30.4 us (13%)
  waiting for transfers between devices  21.6 us (9%)
  between operations  14.6 us (6%)
  local copies, waits for them, and re-layouts  10.1 us (4%)
  other arithmetic  4.8 us (2%)
    psum x4, blocking collectives, by_each_axis(): half = lax.psum(x, axis_one)  58.8 us
    psum x4, blocking collectives, by_each_axis(): return lax.psum(half, axis_two)  45 us
    all_gather x5, blocking collectives, mirror_row(): whole_row = lax.all_gather(top_values, 'lon', axis=0, tiled=True)  44.4 us
    ppermute x10, starting transfers between devices, with_halo(): lax.ppermute(tail, axis, [(i, (i + 1) % count) for i in range(ends)])  17.4 us
    ppermute x10, waiting for transfers between devices, with_halo(): lax.ppermute(tail, axis, [(i, (i + 1) % count) for i in range(ends)])  14.7 us
    ppermute x8, starting transfers between devices, with_halo(): lax.ppermute(head, axis, [((i + 1) % count, i) for i in range(ends)])  13 us
    gather x5, local copies, waits for them, and re-layouts, mirror_row(): return jnp.take(whole_row, fold_partner, axis=0)  8.62 us
    ppermute x8, waiting for transfers between devices, with_halo(): lax.ppermute(head, axis, [((i + 1) % count, i) for i in range(ends)])  6.88 us
  transfers between devices with their start and end apart: 18, of which 7 were waited for; matrix products, arithmetic and copies ran while one was open for 4% of the time, Pallas kernels for 0%

profile of v1, /device:TPU:0, one launch (start us, length us, event | category | flops | bytes accessed | tf_op | source)
XLA Modules:
  0.0 229.7 jit_solution(18013462143507745809)
XLA Ops:
  0.6 1.0 slice.203
  1.6 0.5 collective-permute-start.1
  2.1 0.0 copy-start.1
  2.2 0.1 broadcast_select_fusion
  2.3 4.4 %collective-permute-start.4 = (f32[1,256]{1,0:T(1,128)S(1)}, f32[1,256]{1,0:T(1,128)S(1)}, u32[]{:S(2)}, u32[]{:S(2)}) collective-permute-start(f32[1,256]{1,0:T(1,128)S(1)} %slice.255), channel_id=1, source_target_pairs={{0,8},{8,16},{16,24},{1,9},{9,17},{17,25},{2,10},{10,18},{18,26},{... | collective-permute-start | bytes 3080 | tf_op jit(solution)/shard_map/ppermute | solution.py:22
  6.7 1.3 collective-permute-start.3
  8.0 4.5 %collective-permute-start.5 = (f32[1,256]{1,0:T(1,128)S(1)}, f32[1,256]{1,0:T(1,128)S(1)}, u32[]{:S(2)}, u32[]{:S(2)}) collective-permute-start(f32[1,256]{1,0:T(1,128)S(1)} %get-tuple-element.96), channel_id=1, source_target_pairs={{0,8},{8,16},{16,24},{1,9},{9,17},{17,25},{2,10},{10,18},{18,26},{... | collective-permute-start | bytes 3080 | tf_op jit(solution)/shard_map/ppermute | solution.py:22
  12.6 0.1 fusion.57
  12.7 2.7 %collective-permute-start = (f32[128,1]{1,0:T(8,128)S(1)}, f32[128,1]{1,0:T(8,128)S(1)}, u32[]{:S(2)}, u32[]{:S(2)}) collective-permute-start(f32[128,1]{1,0:T(8,128)S(1)} %get-tuple-element.93), channel_id=1, source_target_pairs={{1,0},{2,1},{3,2},{4,3},{5,4},{6,5},{7,6},{0,7},{9,8},{10,9},{11,1... | collective-permute-start | bytes 1544 | tf_op jit(solution)/shard_map/ppermute | solution.py:24
  15.4 10.3 %all-gather.1 = f32[1,2048]{1,0:T(1,128)S(1)} all-gather(f32[1,256]{1,0:T(1,128)S(1)} %get-tuple-element.96), channel_id=3, replica_groups=mesh['lat'=4,'lon'=8] {'lon'}, dimensions={1}, use_global_device_ids=true | all-gather | bytes 9216 | tf_op jit(solution)/shard_map/all_gather | solution.py:63
  25.7 8.8 %all-gather = f32[1,2048]{1,0:T(1,128)S(1)} all-gather(f32[1,256]{1,0:T(1,128)S(1)} %slice.214), channel_id=2, replica_groups=mesh['lat'=4,'lon'=8] {'lon'}, dimensions={1}, use_global_device_ids=true | all-gather | bytes 9216 | tf_op jit(solution)/shard_map/all_gather | solution.py:63
  34.5 1.7 gather_fusion
  36.2 0.0 copy-start.3
  36.2 1.7 gather_fusion.1
  37.9 0.0 collective-permute-done.1
  37.9 0.4 collective-permute-start.2
  38.4 5.1 %collective-permute-done.2 = f32[128,1]{1,0:T(8,128)S(1)} collective-permute-done((f32[128,1]{1,0:T(8,128)S(1)}, f32[128,1]{1,0:T(8,128)S(1)}, u32[]{:S(2)}, u32[]{:S(2)}) %collective-permute-start.2) | collective-permute-done | bytes 544 | tf_op jit(solution)/shard_map/ppermute | solution.py:22
  43.5 0.0 collective-permute-done.4
  43.5 0.0 collective-permute-done.3
  43.5 0.0 collective-permute-done.5
  43.5 0.2 fusion.35
  43.8 0.7 multiply_reduce_fusion.6
  44.4 14.2 %all-reduce.3 = (f32[]{:T(128)}, f32[]{:T(128)}) all-reduce(f32[]{:T(128)} %get-tuple-element.58, f32[]{:T(128)} %get-tuple-element.57), channel_id=1, replica_groups=mesh['lat'=4,'lon'=8] {'lon'}, use_global_device_ids=true, to_apply=%region_1.2 | all-reduce | flops 2 | bytes 16 | tf_op jit(solution)/shard_map/psum | solution.py:10
  58.6 10.5 %all-reduce.7 = (f32[]{:T(128)}, f32[]{:T(128)}) all-reduce(f32[]{:T(128)} %get-tuple-element.65, f32[]{:T(128)} %get-tuple-element.66), channel_id=1, replica_groups=mesh['lat'=4,'lon'=8] {'lat'}, use_global_device_ids=true, to_apply=%region_2.3 | all-reduce | flops 2 | bytes 16 | tf_op jit(solution)/shard_map/psum | solution.py:11
  70.5 8.4 %all-gather.2 = f32[1,2048]{1,0:T(1,128)S(1)} all-gather(f32[1,256]{1,0:T(1,128)S(1)} %get-tuple-element.92), channel_id=4, replica_groups=mesh['lat'=4,'lon'=8] {'lon'}, dimensions={1}, use_global_device_ids=true | all-gather | bytes 9216 | tf_op jit(solution)/shard_map/all_gather | solution.py:63
  79.0 1.6 collective-permute-start.9
  80.6 0.1 fusion.55
  80.7 1.7 gather_fusion.2
  82.4 1.3 collective-permute-start.8
  83.7 1.7 collective-permute-start.6
  85.4 0.0 collective-permute-start.7
  85.4 2.3 collective-permute-done.6
  87.7 3.2 %collective-permute-done.7 = f32[128,1]{1,0:T(8,128)S(1)} collective-permute-done((f32[128,1]{1,0:T(8,128)S(1)}, f32[128,1]{1,0:T(8,128)S(1)}, u32[]{:S(2)}, u32[]{:S(2)}) %collective-permute-start.7) | collective-permute-done | bytes 544 | tf_op jit(solution)/shard_map/ppermute | solution.py:22
  90.9 0.2 fusion.24
  91.2 0.7 multiply_reduce_fusion.4
  91.9 14.9 %all-reduce.2 = (f32[]{:T(128)}, f32[]{:T(128)}) all-reduce(f32[]{:T(128)} %get-tuple-element.54, f32[]{:T(128)} %get-tuple-element.53), channel_id=1, replica_groups=mesh['lat'=4,'lon'=8] {'lon'}, use_global_device_ids=true, to_apply=%region_7.9 | all-reduce | flops 2 | bytes 16 | tf_op jit(solution)/shard_map/psum | solution.py:10
  106.8 11.9 %all-reduce.6 = (f32[]{:T(128)}, f32[]{:T(128)}) all-reduce(f32[]{:T(128)} %get-tuple-element.63, f32[]{:T(128)} %get-tuple-element.64), channel_id=1, replica_groups=mesh['lat'=4,'lon'=8] {'lat'}, use_global_device_ids=true, to_apply=%region_8.10 | all-reduce | flops 2 | bytes 16 | tf_op jit(solution)/shard_map/psum | solution.py:11
  123.4 0.1 convert_multiply_fusion.1
  123.4 8.4 %all-gather.3 = f32[1,2048]{1,0:T(1,128)S(1)} all-gather(f32[1,256]{1,0:T(1,128)S(1)} %get-tuple-element.88), channel_id=5, replica_groups=mesh['lat'=4,'lon'=8] {'lon'}, dimensions={1}, use_global_device_ids=true | all-gather | bytes 9216 | tf_op jit(solution)/shard_map/all_gather | solution.py:63
  131.9 3.6 %collective-permute-start.13 = (f32[1,256]{1,0:T(1,128)S(1)}, f32[1,256]{1,0:T(1,128)S(1)}, u32[]{:S(2)}, u32[]{:S(2)}) collective-permute-start(f32[1,256]{1,0:T(1,128)S(1)} %get-tuple-element.88), channel_id=1, source_target_pairs={{0,8},{8,16},{16,24},{1,9},{9,17},{17,25},{2,10},{10,18},{18,26},{... | collective-permute-start | bytes 3080 | tf_op jit(solution)/shard_map/ppermute | solution.py:22
  135.5 0.1 fusion.53
  135.6 1.7 gather_fusion.3
  137.3 1.3 collective-permute-start.12
  138.6 1.7 collective-permute-start.10
  140.3 2.3 collective-permute-done.10
  142.6 3.2 %collective-permute-done.11 = f32[128,1]{1,0:T(8,128)S(1)} collective-permute-done((f32[128,1]{1,0:T(8,128)S(1)}, f32[128,1]{1,0:T(8,128)S(1)}, u32[]{:S(2)}, u32[]{:S(2)}) %collective-permute-start.11) | collective-permute-done | bytes 544 | tf_op jit(solution)/shard_map/ppermute | solution.py:22
  145.8 0.2 fusion.13
  146.1 0.7 multiply_reduce_fusion.2
  146.8 14.8 %all-reduce.1 = (f32[]{:T(128)}, f32[]{:T(128)}) all-reduce(f32[]{:T(128)} %get-tuple-element.52, f32[]{:T(128)} %get-tuple-element.51), channel_id=1, replica_groups=mesh['lat'=4,'lon'=8] {'lon'}, use_global_device_ids=true, to_apply=%region_13.15 | all-reduce | flops 2 | bytes 16 | tf_op jit(solution)/shard_map/psum | solution.py:10
  161.6 11.3 %all-reduce.5 = (f32[]{:T(128)}, f32[]{:T(128)}) all-reduce(f32[]{:T(128)} %get-tuple-element.61, f32[]{:T(128)} %get-tuple-element.62), channel_id=1, replica_groups=mesh['lat'=4,'lon'=8] {'lat'}, use_global_device_ids=true, to_apply=%region_14.16 | all-reduce | flops 2 | bytes 16 | tf_op jit(solution)/shard_map/psum | solution.py:11
  176.9 0.1 convert_multiply_fusion
  177.0 8.4 %all-gather.4 = f32[1,2048]{1,0:T(1,128)S(1)} all-gather(f32[1,256]{1,0:T(1,128)S(1)} %get-tuple-element.84), channel_id=6, replica_groups=mesh['lat'=4,'lon'=8] {'lon'}, dimensions={1}, use_global_device_ids=true | all-gather | bytes 9216 | tf_op jit(solution)/shard_map/all_gather | solution.py:63
  185.4 2.2 collective-permute-start.17
  187.7 0.1 fusion.51
  187.8 1.7 gather_fusion.4
  189.5 1.3 collective-permute-start.16
  190.8 1.7 collective-permute-start.14
  192.5 2.3 collective-permute-done.14
  194.8 3.2 %collective-permute-done.15 = f32[128,1]{1,0:T(8,128)S(1)} collective-permute-done((f32[128,1]{1,0:T(8,128)S(1)}, f32[128,1]{1,0:T(8,128)S(1)}, u32[]{:S(2)}, u32[]{:S(2)}) %collective-permute-start.15) | collective-permute-done | bytes 544 | tf_op jit(solution)/shard_map/ppermute | solution.py:22
  198.0 0.2 fusion.2
  198.3 0.7 multiply_reduce_fusion
  198.9 14.9 %all-reduce = (f32[]{:T(128)}, f32[]{:T(128)}) all-reduce(f32[]{:T(128)} %get-tuple-element.56, f32[]{:T(128)} %get-tuple-element.55), channel_id=1, replica_groups=mesh['lat'=4,'lon'=8] {'lon'}, use_global_device_ids=true, to_apply=%region_19.21 | all-reduce | flops 2 | bytes 16 | tf_op jit(solution)/shard_map/psum | solution.py:10
  213.8 11.3 %all-reduce.4 = (f32[]{:T(128)}, f32[]{:T(128)}) all-reduce(f32[]{:T(128)} %get-tuple-element.59, f32[]{:T(128)} %get-tuple-element.60), channel_id=1, replica_groups=mesh['lat'=4,'lon'=8] {'lat'}, use_global_device_ids=true, to_apply=%region_20.22 | all-reduce | flops 2 | bytes 16 | tf_op jit(solution)/shard_map/psum | solution.py:11
  228.8 0.9 multiply_subtract_fusion
  (42 shorter events, 0.4 us)
Async XLA Ops:
  0.6 1.5 copy-start.4
  1.6 36.3 %collective-permute-start.1 = (f32[128,1]{1,0:T(8,128)S(1)}, f32[128,1]{1,0:T(8,128)S(1)}, u32[]{:S(2)}, u32[]{:S(2)}) collective-permute-start(f32[128,1]{1,0:T(8,128)S(1)} %slice.203), channel_id=1, source_target_pairs={{0,1},{1,2},{2,3},{3,4},{4,5},{5,6},{6,7},{7,0},{8,9},{9,10},{10,1... | collective-permute-start | bytes 1544 | tf_op jit(solution)/shard_map/ppermute | solution.py:22
  2.1 4.5 %copy-start = (s32[128,256]{1,0:T(8,128)S(1)}, s32[128,256]{1,0:T(8,128)}, u32[]{:S(2)}) copy-start(s32[128,256]{1,0:T(8,128)} %param.20) | copy-start | bytes 393220
  2.1 4.6 %copy-start.1 = (f32[128,256]{1,0:T(8,128)S(1)}, f32[128,256]{1,0:T(8,128)}, u32[]{:S(2)}) copy-start(f32[128,256]{1,0:T(8,128)} %param.16) | copy-start | bytes 393220
  2.3 41.2 %collective-permute-start.4 = (f32[1,256]{1,0:T(1,128)S(1)}, f32[1,256]{1,0:T(1,128)S(1)}, u32[]{:S(2)}, u32[]{:S(2)}) collective-permute-start(f32[1,256]{1,0:T(1,128)S(1)} %slice.255), channel_id=1, source_target_pairs={{0,8},{8,16},{16,24},{1,9},{9,17},{17,25},{2,10},{10,18},{18,26},{... | collective-permute-start | bytes 3080 | tf_op jit(solution)/shard_map/ppermute | solution.py:22
  6.7 36.7 %collective-permute-start.3 = (f32[1,256]{1,0:T(1,128)S(1)}, f32[1,256]{1,0:T(1,128)S(1)}, u32[]{:S(2)}, u32[]{:S(2)}) collective-permute-start(f32[1,256]{1,0:T(1,128)S(1)} %get-tuple-element.95), channel_id=1, source_target_pairs={{8,0},{16,8},{24,16},{9,1},{17,9},{25,17},{10,2},{18,10},{26,18},{... | collective-permute-start | bytes 3080 | tf_op jit(solution)/shard_map/ppermute | solution.py:24
  8.0 35.5 %collective-permute-start.5 = (f32[1,256]{1,0:T(1,128)S(1)}, f32[1,256]{1,0:T(1,128)S(1)}, u32[]{:S(2)}, u32[]{:S(2)}) collective-permute-start(f32[1,256]{1,0:T(1,128)S(1)} %get-tuple-element.96), channel_id=1, source_target_pairs={{0,8},{8,16},{16,24},{1,9},{9,17},{17,25},{2,10},{10,18},{18,26},{... | collective-permute-start | bytes 3080 | tf_op jit(solution)/shard_map/ppermute | solution.py:22
  12.7 25.7 %collective-permute-start = (f32[128,1]{1,0:T(8,128)S(1)}, f32[128,1]{1,0:T(8,128)S(1)}, u32[]{:S(2)}, u32[]{:S(2)}) collective-permute-start(f32[128,1]{1,0:T(8,128)S(1)} %get-tuple-element.93), channel_id=1, source_target_pairs={{1,0},{2,1},{3,2},{4,3},{5,4},{6,5},{7,6},{0,7},{9,8},{10,9},{11,1... | collective-permute-start | bytes 1544 | tf_op jit(solution)/shard_map/ppermute | solution.py:24
  15.4 10.3 %copy-start.5 = (s32[256]{0:T(256)S(1)}, s32[256]{0:T(256)}, u32[]{:S(2)}) copy-start(s32[256]{0:T(256)} %param.21) | copy-start | bytes 3076
  36.2 7.3 %copy-start.3 = (f32[128,256]{1,0:T(8,128)S(1)}, f32[128,256]{1,0:T(8,128)}, u32[]{:S(2)}) copy-start(f32[128,256]{1,0:T(8,128)} %param.18) | copy-start | bytes 393220
  37.9 5.5 %collective-permute-start.2 = (f32[128,1]{1,0:T(8,128)S(1)}, f32[128,1]{1,0:T(8,128)S(1)}, u32[]{:S(2)}, u32[]{:S(2)}) collective-permute-start(f32[128,1]{1,0:T(8,128)S(1)} %get-tuple-element.94), channel_id=1, source_target_pairs={{0,1},{1,2},{2,3},{3,4},{4,5},{5,6},{6,7},{7,0},{8,9},{9,10},{10,1... | collective-permute-start | bytes 1544 | tf_op jit(solution)/shard_map/ppermute | solution.py:22
  38.3 5.4 %copy-start.2 = (f32[128,256]{1,0:T(8,128)S(1)}, f32[128,256]{1,0:T(8,128)}, u32[]{:S(2)}) copy-start(f32[128,256]{1,0:T(8,128)} %param.17) | copy-start | bytes 393220
  79.0 12.0 %collective-permute-start.9 = (f32[1,256]{1,0:T(1,128)S(1)}, f32[1,256]{1,0:T(1,128)S(1)}, u32[]{:S(2)}, u32[]{:S(2)}) collective-permute-start(f32[1,256]{1,0:T(1,128)S(1)} %get-tuple-element.92), channel_id=1, source_target_pairs={{0,8},{8,16},{16,24},{1,9},{9,17},{17,25},{2,10},{10,18},{18,26},{... | collective-permute-start | bytes 3080 | tf_op jit(solution)/shard_map/ppermute | solution.py:22
  82.4 8.5 %collective-permute-start.8 = (f32[1,256]{1,0:T(1,128)S(1)}, f32[1,256]{1,0:T(1,128)S(1)}, u32[]{:S(2)}, u32[]{:S(2)}) collective-permute-start(f32[1,256]{1,0:T(1,128)S(1)} %get-tuple-element.91), channel_id=1, source_target_pairs={{8,0},{16,8},{24,16},{9,1},{17,9},{25,17},{10,2},{18,10},{26,18},{... | collective-permute-start | bytes 3080 | tf_op jit(solution)/shard_map/ppermute | solution.py:24
  83.7 4.0 %collective-permute-start.6 = (f32[128,1]{1,0:T(8,128)S(1)}, f32[128,1]{1,0:T(8,128)S(1)}, u32[]{:S(2)}, u32[]{:S(2)}) collective-permute-start(f32[128,1]{1,0:T(8,128)S(1)} %get-tuple-element.89), channel_id=1, source_target_pairs={{1,0},{2,1},{3,2},{4,3},{5,4},{6,5},{7,6},{0,7},{9,8},{10,9},{11,1... | collective-permute-start | bytes 1544 | tf_op jit(solution)/shard_map/ppermute | solution.py:24
  85.4 5.5 %collective-permute-start.7 = (f32[128,1]{1,0:T(8,128)S(1)}, f32[128,1]{1,0:T(8,128)S(1)}, u32[]{:S(2)}, u32[]{:S(2)}) collective-permute-start(f32[128,1]{1,0:T(8,128)S(1)} %get-tuple-element.90), channel_id=1, source_target_pairs={{0,1},{1,2},{2,3},{3,4},{4,5},{5,6},{6,7},{7,0},{8,9},{9,10},{10,1... | collective-permute-start | bytes 1544 | tf_op jit(solution)/shard_map/ppermute | solution.py:22
  131.9 13.9 %collective-permute-start.13 = (f32[1,256]{1,0:T(1,128)S(1)}, f32[1,256]{1,0:T(1,128)S(1)}, u32[]{:S(2)}, u32[]{:S(2)}) collective-permute-start(f32[1,256]{1,0:T(1,128)S(1)} %get-tuple-element.88), channel_id=1, source_target_pairs={{0,8},{8,16},{16,24},{1,9},{9,17},{17,25},{2,10},{10,18},{18,26},{... | collective-permute-start | bytes 3080 | tf_op jit(solution)/shard_map/ppermute | solution.py:22
  137.3 8.5 %collective-permute-start.12 = (f32[1,256]{1,0:T(1,128)S(1)}, f32[1,256]{1,0:T(1,128)S(1)}, u32[]{:S(2)}, u32[]{:S(2)}) collective-permute-start(f32[1,256]{1,0:T(1,128)S(1)} %get-tuple-element.87), channel_id=1, source_target_pairs={{8,0},{16,8},{24,16},{9,1},{17,9},{25,17},{10,2},{18,10},{26,18},{... | collective-permute-start | bytes 3080 | tf_op jit(solution)/shard_map/ppermute | solution.py:24
  138.6 4.0 %collective-permute-start.10 = (f32[128,1]{1,0:T(8,128)S(1)}, f32[128,1]{1,0:T(8,128)S(1)}, u32[]{:S(2)}, u32[]{:S(2)}) collective-permute-start(f32[128,1]{1,0:T(8,128)S(1)} %get-tuple-element.85), channel_id=1, source_target_pairs={{1,0},{2,1},{3,2},{4,3},{5,4},{6,5},{7,6},{0,7},{9,8},{10,9},{11,1... | collective-permute-start | bytes 1544 | tf_op jit(solution)/shard_map/ppermute | solution.py:24
  140.3 5.5 %collective-permute-start.11 = (f32[128,1]{1,0:T(8,128)S(1)}, f32[128,1]{1,0:T(8,128)S(1)}, u32[]{:S(2)}, u32[]{:S(2)}) collective-permute-start(f32[128,1]{1,0:T(8,128)S(1)} %get-tuple-element.86), channel_id=1, source_target_pairs={{0,1},{1,2},{2,3},{3,4},{4,5},{5,6},{6,7},{7,0},{8,9},{9,10},{10,1... | collective-permute-start | bytes 1544 | tf_op jit(solution)/shard_map/ppermute | solution.py:22
  185.4 12.6 %collective-permute-start.17 = (f32[1,256]{1,0:T(1,128)S(1)}, f32[1,256]{1,0:T(1,128)S(1)}, u32[]{:S(2)}, u32[]{:S(2)}) collective-permute-start(f32[1,256]{1,0:T(1,128)S(1)} %get-tuple-element.84), channel_id=1, source_target_pairs={{0,8},{8,16},{16,24},{1,9},{9,17},{17,25},{2,10},{10,18},{18,26},{... | collective-permute-start | bytes 3080 | tf_op jit(solution)/shard_map/ppermute | solution.py:22
  189.5 8.5 %collective-permute-start.16 = (f32[1,256]{1,0:T(1,128)S(1)}, f32[1,256]{1,0:T(1,128)S(1)}, u32[]{:S(2)}, u32[]{:S(2)}) collective-permute-start(f32[1,256]{1,0:T(1,128)S(1)} %get-tuple-element.83), channel_id=1, source_target_pairs={{8,0},{16,8},{24,16},{9,1},{17,9},{25,17},{10,2},{18,10},{26,18},{... | collective-permute-start | bytes 3080 | tf_op jit(solution)/shard_map/ppermute | solution.py:24
  190.8 4.0 %collective-permute-start.14 = (f32[128,1]{1,0:T(8,128)S(1)}, f32[128,1]{1,0:T(8,128)S(1)}, u32[]{:S(2)}, u32[]{:S(2)}) collective-permute-start(f32[128,1]{1,0:T(8,128)S(1)} %get-tuple-element.81), channel_id=1, source_target_pairs={{1,0},{2,1},{3,2},{4,3},{5,4},{6,5},{7,6},{0,7},{9,8},{10,9},{11,1... | collective-permute-start | bytes 1544 | tf_op jit(solution)/shard_map/ppermute | solution.py:24
  192.5 5.5 %collective-permute-start.15 = (f32[128,1]{1,0:T(8,128)S(1)}, f32[128,1]{1,0:T(8,128)S(1)}, u32[]{:S(2)}, u32[]{:S(2)}) collective-permute-start(f32[128,1]{1,0:T(8,128)S(1)} %get-tuple-element.82), channel_id=1, source_target_pairs={{0,1},{1,2},{2,3},{3,4},{4,5},{5,6},{6,7},{7,0},{8,9},{9,10},{10,1... | collective-permute-start | bytes 1544 | tf_op jit(solution)/shard_map/ppermute | solution.py:22
